TPU v7x, 32 devices: a whole 2x2x4 slice. The times are simulated.
32 devices in a mesh: grp: 4 (over x, core), ep: 4 (over z), sq: 2 (over y).
Axes of the slice: x: 2, y: 2, z: 4, core: 2. Of those that a mesh axis runs over, the one named last changes fastest.
Arguments:
- queries: bfloat16 [8192, 2048], P(('grp', 'ep', 'sq')), may hold values from -32 to 32
- keys: bfloat16 [8192, 512], P(('grp', 'ep', 'sq')), may hold values from -32 to 32
- values: bfloat16 [8192, 512], P(('grp', 'ep', 'sq')), may hold values from -6 to 6
- norm_gain: float32 [2048], replicated, may hold values from 0.1 to 1.9
- expert_ids: int32 [8192, 2], P(('grp', 'ep', 'sq')), may hold values from 0 to 3, all different within a row; in each aligned block of 256 rows (0 to 255, 256 to 511, ...) at most 192 rows name the same one
- gate_values: float32 [8192, 2], P(('grp', 'ep', 'sq')), may hold values from 0.1 to 1
- hidden_grad: bfloat16 [8192, 1024], P(('grp', 'ep', 'sq')), may hold values from -0.59765625 to 0.59765625
- gate_weight: bfloat16 [4, 2048, 1024], P('ep', None, 'sq'), may hold values from -0.125 to 0.125
- up_weight: bfloat16 [4, 2048, 1024], P('ep', None, 'sq'), may hold values from -0.125 to 0.125
Outputs:
- gate_grad: float32 [4, 2048, 1024], P('ep', 'grp', 'sq')
Inputs may be any that keep to these rules, and one draw needn't show every extreme that they name: `expert_ids`: each token names 2 different experts; within the 256 tokens of one device no expert is named more than 192 times.
All inputs are finite; a program needn't handle non-finite values.
Results may differ from a plain program's by a relative error of at most 0.0085.
Values may be sent and summed in bfloat16 or wider, within the bound.
A program may use at most 64 MiB of HBM per device.

v0:
```python
import math
import jax
import jax.numpy as jnp
from jax import lax
from jax.sharding import PartitionSpec as P

HEAD_DIM = 128
LENGTH = 512
epsilon = 1e-05
masked_score = -1e30


def gate_term(inputs, cotangent, weight_gate, weight_up):
    pre_gate = jnp.dot(inputs, weight_gate, preferred_element_type=jnp.float32)
    pre_up = jnp.dot(inputs, weight_up, preferred_element_type=jnp.float32)
    sigmoid_gate = jax.nn.sigmoid(pre_gate)
    slope = sigmoid_gate * (1.0 + pre_gate * (1.0 - sigmoid_gate))
    delta_gate = (cotangent.astype(jnp.float32) * pre_up * slope).astype(jnp.bfloat16)
    return lax.dot_general(
        inputs, delta_gate, (((0,), (0,)), ((), ())), preferred_element_type=jnp.float32
    )


def body(
    queries, keys, values, norm_gain, expert_ids, gate_values, hidden_grad, gate_weight, up_weight
):
    rows_here, model_width = queries.shape
    kv_width = keys.shape[1]
    kv_heads = kv_width // HEAD_DIM
    group_size = model_width // kv_width
    score_scale = 1.0 / math.sqrt(HEAD_DIM)
    shard_index = lax.axis_index("sq")
    query_positions = shard_index * rows_here + jnp.arange(rows_here, dtype=jnp.int32)
    query_sequence = query_positions // LENGTH
    query_heads = queries.reshape(rows_here, kv_heads, group_size, HEAD_DIM)
    running_max = jnp.full((rows_here, kv_heads, group_size), masked_score, jnp.float32)
    key_rows = lax.all_gather(keys, "sq", axis=0, tiled=True)
    value_rows = lax.all_gather(values, "sq", axis=0, tiled=True)
    key_count = key_rows.shape[0]
    key_heads = key_rows.reshape(key_count, kv_heads, HEAD_DIM)
    value_heads = value_rows.reshape(key_count, kv_heads, HEAD_DIM)
    scores = (
        jnp.einsum("tkgd,rkd->tkgr", query_heads, key_heads, preferred_element_type=jnp.float32)
        * score_scale
    )
    key_positions = jnp.arange(key_count, dtype=jnp.int32)
    causal = key_positions[None, :] <= query_positions[:, None]
    same_sequence = (key_positions // LENGTH)[None, :] == query_sequence[:, None]
    allowed = (causal & same_sequence)[:, None, None, :]
    scores = jnp.where(allowed, scores, masked_score)
    updated_max = jnp.maximum(running_max, jnp.max(scores, axis=-1))
    exponent_terms = jnp.where(allowed, jnp.exp(scores - updated_max[..., None]), 0.0)
    running_sum = jnp.sum(exponent_terms, axis=-1)
    running_out = jnp.einsum(
        "tkgr,rkd->tkgd",
        exponent_terms.astype(jnp.bfloat16),
        value_heads,
        preferred_element_type=jnp.float32,
    )
    attended = (running_out / running_sum[..., None]).reshape(rows_here, model_width)
    mean_square = jnp.mean(attended * attended, axis=-1, keepdims=True)
    normed = (attended * lax.rsqrt(mean_square + epsilon) * norm_gain).astype(jnp.bfloat16)
    top_count = expert_ids.shape[1]
    experts = lax.axis_size("ep")
    capacity = rows_here * top_count // experts * 3 // 2
    hidden_width = hidden_grad.shape[1]
    flat_ids = expert_ids.reshape(-1)
    one_hot = (flat_ids[:, None] == jnp.arange(experts, dtype=jnp.int32)[None, :]).astype(jnp.int32)
    slot_rank = jnp.sum(jnp.cumsum(one_hot, axis=0) * one_hot, axis=1) - 1
    slot_target = flat_ids * capacity + slot_rank
    routed_inputs = jnp.repeat(normed, top_count, axis=0)
    routed_grad = (
        gate_values.reshape(-1, 1) * jnp.repeat(hidden_grad, top_count, axis=0).astype(jnp.float32)
    ).astype(jnp.bfloat16)
    send_inputs = (
        jnp.zeros((experts * capacity, model_width), jnp.bfloat16)
        .at[slot_target]
        .set(routed_inputs)
    )
    send_grad = (
        jnp.zeros((experts * capacity, hidden_width), jnp.bfloat16).at[slot_target].set(routed_grad)
    )
    send_inputs = send_inputs.reshape(experts, capacity, model_width)
    send_grad = send_grad.reshape(experts, capacity, hidden_width)
    got_inputs, got_grad = (
        lax.all_to_all(send_inputs, "ep", split_axis=0, concat_axis=0, tiled=True),
        lax.all_to_all(send_grad, "ep", split_axis=0, concat_axis=0, tiled=True),
    )
    expert_inputs = got_inputs.reshape(-1, model_width)
    expert_grad = got_grad.reshape(-1, hidden_width)
    weight_gate = gate_weight[0]
    weight_up = up_weight[0]
    local_hidden = weight_gate.shape[1]
    column_start = shard_index * local_hidden
    input_rows = lax.all_gather(expert_inputs, "sq", axis=0, tiled=True)
    grad_rows = lax.all_gather(expert_grad, "sq", axis=0, tiled=True)
    cotangent = lax.dynamic_slice_in_dim(grad_rows, column_start, local_hidden, 1)
    summed = gate_term(input_rows, cotangent, weight_gate, weight_up)
    return lax.psum_scatter(
        summed[None].astype(jnp.bfloat16), "grp", scatter_dimension=1, tiled=True
    ).astype(jnp.float32)


def solution(mesh):
    return jax.shard_map(
        body,
        mesh=mesh,
        in_specs=(
            P(("grp", "ep", "sq"), None),
            P(("grp", "ep", "sq"), None),
            P(("grp", "ep", "sq"), None),
            P(),
            P(("grp", "ep", "sq"), None),
            P(("grp", "ep", "sq"), None),
            P(("grp", "ep", "sq"), None),
            P("ep", None, "sq"),
            P("ep", None, "sq"),
        ),
        out_specs=P("ep", "grp", "sq"),
        check_vma=False,
    )
```

profile of v0, /device:TPU:0, one launch (start us, length us, event | category | flops | bytes accessed | tf_op | source)
XLA Modules:
  0.0 312.1 jit_solution(6690040816627483020)
XLA Ops:
  6.5 0.0 copy-start
  6.5 0.0 all-gather.3.cloned.1.call-start
  6.5 0.8 broadcast_multiply_fusion
  7.4 0.8 copy.15
  8.2 0.1 eq.46
  8.3 0.1 eq.42
  8.5 0.1 copy.14
  8.6 0.1 mul.78
  8.8 1.2 reduce-window.6
  10.0 0.2 slice_reduce_fusion
  10.2 0.2 reduce-window.9
  10.4 0.1 add_bitcast_fusion
  10.5 1.1 copy.17
  11.6 10.0 %all_gather.12 = bf16[512,512]{0,1:T(8,128)(2,1)} all-gather(bf16[256,512]{0,1:T(8,128)(2,1)S(1)} %copy.17), channel_id=1, replica_groups=mesh['grp'=4,'ep'=4,'sq'=2] {'sq'}, dimensions={0}, use_global_device_ids=true | all-gather | bytes 786432 | tf_op jit(solution)/shard_map/all_gather | solution.py:37
  21.7 8.4 %all_gather.13 = bf16[512,512]{1,0:T(8,128)(2,1)S(1)} all-gather(bf16[256,512]{1,0:T(8,128)(2,1)} %param.11), channel_id=1, replica_groups=mesh['grp'=4,'ep'=4,'sq'=2] {'sq'}, dimensions={0}, use_global_device_ids=true | all-gather | bytes 786432 | tf_op jit(solution)/shard_map/all_gather | solution.py:38
  30.0 1.0 copy.20
  31.0 1.8 reshape.173
  32.8 0.2 fusion.25
  33.0 2.7 fusion
  35.8 0.0 copy-start.2
  35.8 2.0 fusion.1
  37.8 0.0 copy-start.3
  37.8 2.5 multiply_reduce_fusion
  40.3 1.3 fusion.13
  41.7 1.5 copy.22
  43.1 2.6 broadcast_in_dim.51
  45.8 4.1 %reshape.185 = bf16[512,2048]{1,0:T(8,128)(2,1)} reshape(bf16[256,2,2048]{2,1,0:T(2,128)(2,1)} %broadcast_in_dim.51) | data formatting | bytes 4194304 | tf_op jit(solution)/shard_map/reshape | solution.py:71
  49.9 6.7 %scatter_custom_fusion = bf16[768,2048]{1,0:T(8,128)(2,1)} fusion(s32[512]{0:T(512)S(1)} %bitcast.79, bf16[512,2048]{1,0:T(8,128)(2,1)} %reshape.185, bf16[]{:T(256)} %constant.25.clone.1), kind=kCustom, calls=%fused_computation.23 | custom fusion | bytes 3146240 | tf_op jit(solution)/shard_map/scatter | solution.py:78
  56.6 74.8 %all_to_all.10 = bf16[4,192,2048]{2,1,0:T(8,128)(2,1)} all-to-all(bf16[4,192,2048]{2,1,0:T(8,128)(2,1)} %bitcast.72), channel_id=1, replica_groups=mesh['grp'=4,'ep'=4,'sq'=2] {'ep'}, dimensions={0} | all-to-all | bytes 6291456 | tf_op jit(solution)/shard_map/all_to_all | solution.py:86
  131.4 0.0 all-gather.3.cloned.1.call-update
  131.4 0.0 all-gather.5.cloned.1.call-start
  131.5 0.6 copy-done.4
  132.1 0.1 copy.23
  132.2 0.1 mul.89
  132.4 0.1 copy-done.1
  132.5 2.0 broadcast_in_dim.53
  134.4 3.7 %convert_element_type.40 = f32[512,1024]{1,0:T(8,128)} reshape(f32[256,2,1024]{2,1,0:T(2,128)} %broadcast_in_dim.53) | data formatting | bytes 4194304 | tf_op jit(solution)/shard_map/convert_element_type | solution.py:73
  138.1 5.3 %scatter_custom_fusion.1 = bf16[768,1024]{1,0:T(8,128)(2,1)} fusion(s32[512]{0:T(512)S(1)} %bitcast.80, f32[512,1024]{1,0:T(8,128)} %convert_element_type.40, f32[512]{0:T(512)S(1)} %mul.89, bf16[]{:T(256)} %constant.25.clone.1), kind=kCustom, calls=%fused_computation.25 | custom fusion | flops 1048576 | bytes 3672066 | tf_op jit(solution)/shard_map/scatter | solution.py:81
  143.4 40.3 %all_to_all.11 = bf16[4,192,1024]{2,1,0:T(8,128)(2,1)} all-to-all(bf16[4,192,1024]{2,1,0:T(8,128)(2,1)} %bitcast.74), channel_id=1, replica_groups=mesh['grp'=4,'ep'=4,'sq'=2] {'ep'}, dimensions={0} | all-to-all | bytes 3145728 | tf_op jit(solution)/shard_map/all_to_all | solution.py:87
  183.7 0.0 all-gather.5.cloned.1.call-update
  183.7 0.0 reduce-scatter.2.cloned.1.call-start
  183.7 26.9 %all-gather.3.cloned.1.call-done = bf16[1536,2048]{1,0:T(8,128)(2,1)} async-done(((bf16[768,2048]{1,0:T(8,128)(2,1)}), bf16[1536,2048]{1,0:T(8,128)(2,1)}) %all-gather.3.cloned.1.call-update) | async-done | bytes 6291472 | tf_op jit(solution)/shard_map/all_gather | solution.py:95
  210.7 8.5 %fusion.9 = f32[1536,512]{1,0:T(8,128)} fusion(bf16[1536,2048]{1,0:T(8,128)(2,1)} %all-gather.3.cloned.1.call-done, bf16[1,2048,512]{2,1,0:T(8,128)(2,1)} %param.16), kind=kOutput, calls=%fused_computation.14 | convolution fusion | flops 3221225472 | bytes 11534336 | tf_op jit(solution)/shard_map/dot_general | solution.py:14
  219.2 38.0 %all-gather.5.cloned.1.call-done = bf16[1536,1024]{1,0:T(8,128)(2,1)} async-done(((bf16[768,1024]{1,0:T(8,128)(2,1)}), bf16[1536,1024]{1,0:T(8,128)(2,1)}) %all-gather.5.cloned.1.call-update) | async-done | bytes 3145744 | tf_op jit(solution)/shard_map/all_gather | solution.py:96
  257.2 14.6 %fusion.8 = bf16[1,2048,512]{2,1,0:T(8,128)(2,1)} fusion(bf16[1536,2048]{1,0:T(8,128)(2,1)} %all-gather.3.cloned.1.call-done, f32[1536,512]{1,0:T(8,128)} %fusion.9, bf16[1,2048,512]{2,1,0:T(8,128)(2,1)S(1)} %copy-done, bf16[1536,1024]{1,0:T(8,128)(2,1)} %all-gather.5.cloned.1.call-done, s32[]{:T(128)S(6)} %select_n.44), kind=kOutput, calls=%fused_computation.13 | convolution fusion | flops 6452150272 | bytes 21495812 | tf_op jit(solution)/shard_map/dot_general | solution.py:19
  271.8 0.0 reduce-scatter.2.cloned.1.call-update
  271.8 31.6 %reduce-scatter.2.cloned.1.call-done = bf16[1,512,512]{2,1,0:T(8,128)(2,1)} async-done(((bf16[1,2048,512]{2,1,0:T(8,128)(2,1)}), bf16[1,512,512]{2,1,0:T(8,128)(2,1)}) %reduce-scatter.2.cloned.1.call-update) | async-done | bytes 524304 | tf_op jit(solution)/shard_map/reduce_scatter | solution.py:99
  303.4 2.1 convert_element_type.46
  (13 shorter events, 0.1 us)
Async XLA Ops:
  6.5 250.7 %copy-start = (bf16[1,2048,512]{2,1,0:T(8,128)(2,1)S(1)}, bf16[1,2048,512]{2,1,0:T(8,128)(2,1)}, u32[]{:S(2)}) copy-start(bf16[1,2048,512]{2,1,0:T(8,128)(2,1)} %param.17) | copy-start | bytes 6291460
  6.5 204.1 %all-gather.3.cloned.1.call-start = ((), (), s32[]{:S(2)}) async-start(), calls=%async_computation.3 | async-start | bytes 9437184 | tf_op jit(solution)/shard_map/all_gather | solution.py:95
  35.8 2.0 copy-start.2
  37.8 2.5 copy-start.3
  131.4 0.7 copy-start.4
  131.4 1.1 copy-start.1
  131.4 125.8 %all-gather.5.cloned.1.call-start = ((), (), s32[]{:S(2)}) async-start(), calls=%async_computation.4 | async-start | bytes 4718592 | tf_op jit(solution)/shard_map/all_gather | solution.py:96
  183.7 119.7 %reduce-scatter.2.cloned.1.call-start = ((), (), s32[]{:S(2)}) async-start(), calls=%async_computation.5 | async-start | bytes 2621440 | tf_op jit(solution)/shard_map/reduce_scatter | solution.py:99
Sparse Core Ops, SparseCore 0:
  131.6 79.0 all-gather.2
  212.2 44.9 all-gather.4
  272.0 31.4 reduce-scatter.1
where the time goes:
time: 313 us; the launch traced here: 312 us
  blocking collectives  133 us (42%)
  waiting for transfers between devices  96.5 us (31%)
  matrix products  28.4 us (9%)
  local copies, waits for them, and re-layouts  27 us (9%)
  other arithmetic  13.3 us (4%)
  between operations  13.3 us (4%)
    all_to_all x1, blocking collectives, body(): lax.all_to_all(send_inputs, 'ep', split_axis=0, concat_axis=0, tiled=True)  74.8 us
    all_to_all x1, blocking collectives, body(): lax.all_to_all(send_grad, 'ep', split_axis=0, concat_axis=0, tiled=True)  40.3 us
    all_gather x1, waiting for transfers between devices, body(): grad_rows = lax.all_gather(expert_grad, 'sq', axis=0, tiled=True)  38 us
    reduce_scatter x1, waiting for transfers between devices, body(): lax.psum_scatter(summed[None].astype(jnp.bfloat16), 'grp', scatter_dimens...  31.6 us
    all_gather x1, waiting for transfers between devices, body(): input_rows = lax.all_gather(expert_inputs, 'sq', axis=0, tiled=True)  26.9 us
    dot_general x1, matrix products, gate_term(): lax.dot_general(inputs, delta_gate, (((0,), (0,)), ((), ())), preferred_e...  14.6 us
    all_gather x1, blocking collectives, body(): key_rows = lax.all_gather(keys, 'sq', axis=0, tiled=True)  10 us
    dot_general x1, matrix products, gate_term(): pre_gate = jnp.dot(inputs, weight_gate, preferred_element_type=jnp.float32)  8.55 us
  transfers between devices with their start and end apart: 3, of which 3 were waited for; matrix products, arithmetic and copies ran while one was open for 6% of the time, Pallas kernels for 0%

commit v1 on v0

--- a/solution.py
+++ b/solution.py
@@ -35,7 +35,9 @@
     query_heads = queries.reshape(rows_here, kv_heads, group_size, HEAD_DIM)
     running_max = jnp.full((rows_here, kv_heads, group_size), masked_score, jnp.float32)
     key_rows = lax.all_gather(keys, "sq", axis=0, tiled=True)
-    value_rows = lax.all_gather(values, "sq", axis=0, tiled=True)
+    value_rows = jnp.concatenate(
+        lax.all_to_all(jnp.stack([values] * lax.axis_size("sq")), "sq", 0, 0), axis=0
+    )
     key_count = key_rows.shape[0]
     key_heads = key_rows.reshape(key_count, kv_heads, HEAD_DIM)
     value_heads = value_rows.reshape(key_count, kv_heads, HEAD_DIM)

time: 313 us -> 315 us (level)
  blocking collectives: 133 us -> 127 us
  starting transfers between devices: 0.09 us -> 4.35 us
    all_gather x1 -> x0, blocking collectives: 8.37 us -> none  [body(): value_rows = lax.all_gather(values, 'sq', axis=0, tiled=True)]
    all_to_all x0 -> x1, starting transfers between devices: none -> 4.23 us  [body(): lax.all_to_all(jnp.stack([values] * lax.axis_size('sq')), 'sq', 0, 0)]
  transfers between devices with their start and end apart: 3 -> 4, of which waited for: 3 -> 3; matrix products, arithmetic and copies ran while one was open for 6% -> 10% of each run, Pallas kernels for 0% -> 0%
where the time goes in v1:
time: 315 us
  blocking collectives  127 us (40%)
  waiting for transfers between devices  95.2 us (30%)
  matrix products  30.6 us (10%)
  local copies, waits for them, and re-layouts  28.5 us (9%)
  other arithmetic  15.2 us (5%)
  between operations  13.3 us (4%)
  starting transfers between devices  4.35 us (1%)
    all_to_all x1, blocking collectives, body(): lax.all_to_all(send_inputs, 'ep', split_axis=0, concat_axis=0, tiled=True)  76.1 us
    all_to_all x1, blocking collectives, body(): lax.all_to_all(send_grad, 'ep', split_axis=0, concat_axis=0, tiled=True)  40.9 us
    all_gather x1, waiting for transfers between devices, body(): grad_rows = lax.all_gather(expert_grad, 'sq', axis=0, tiled=True)  38 us
    reduce_scatter x1, waiting for transfers between devices, body(): lax.psum_scatter(summed[None].astype(jnp.bfloat16), 'grp', scatter_dimens...  31.6 us
    all_gather x1, waiting for transfers between devices, body(): input_rows = lax.all_gather(expert_inputs, 'sq', axis=0, tiled=True)  25.6 us
    dot_general x1, matrix products, gate_term(): lax.dot_general(inputs, delta_gate, (((0,), (0,)), ((), ())), preferred_e...  14.6 us
    all_gather x1, blocking collectives, body(): key_rows = lax.all_gather(keys, 'sq', axis=0, tiled=True)  10.5 us
    dot_general x1, matrix products, gate_term(): pre_gate = jnp.dot(inputs, weight_gate, preferred_element_type=jnp.float32)  8.55 us
  transfers between devices with their start and end apart: 4, of which 3 were waited for; matrix products, arithmetic and copies ran while one was open for 10% of the time, Pallas kernels for 0%

profile of v1, /device:TPU:0, one launch (start us, length us, event | category | flops | bytes accessed | tf_op | source)
XLA Modules:
  0.0 314.6 jit_solution(3002747873878759565)
XLA Ops:
  6.5 2.0 pad_maximum_fusion
  8.6 4.2 %all-to-all-start = ((bf16[2,256,512]{2,1,0:T(8,128)(2,1)}), bf16[2,256,512]{2,1,0:T(8,128)(2,1)}, u32[]{:S(2)}, u32[]{:S(2)}) async-start(bf16[2,256,512]{2,1,0:T(8,128)(2,1)} %pad_maximum_fusion), calls=%async_computation | async-start | bytes 1048576 | tf_op jit(solution)/shard_map/all_to_all | solution.py:39
  12.8 0.0 all-gather.3.cloned.1.call-start
  12.8 0.7 broadcast_multiply_fusion
  13.5 0.8 copy.15
  14.3 0.1 eq.46
  14.5 0.1 eq.42
  14.7 1.2 reduce-window.6
  15.9 0.2 slice_reduce_fusion
  16.1 0.2 reduce-window.9
  16.3 0.1 add_bitcast_fusion
  16.4 1.1 copy.18
  17.5 10.5 %all_gather.9 = bf16[512,512]{0,1:T(8,128)(2,1)} all-gather(bf16[256,512]{0,1:T(8,128)(2,1)S(1)} %copy.18), channel_id=1, replica_groups=mesh['grp'=4,'ep'=4,'sq'=2] {'sq'}, dimensions={0}, use_global_device_ids=true | all-gather | bytes 786432 | tf_op jit(solution)/shard_map/all_gather | solution.py:37
  28.0 1.8 reshape.170
  29.8 0.2 fusion.26
  29.9 2.7 fusion
  32.7 2.0 fusion.1
  34.8 1.1 copy-done.1
  35.9 0.1 copy.14
  36.0 0.1 mul.78
  36.2 1.2 reshape.195
  37.4 0.0 copy-start.3
  37.4 4.7 %multiply_reduce_fusion = (f32[256]{0:T(256)S(1)}, f32[256,4,4,128]{0,3,2,1:T(8,128)S(1)}) fusion(f32[256,4,4]{0,2,1:T(4,128)S(1)} %fusion.1, f32[4,512,256,4]{2,1,3,0:T(8,128)} %copy-done.1, f32[256,4,4]{0,2,1:T(4,128)S(1)} %broadcast_maximum_fusion, pred[256,512]{0,1:T(8,128)(4,1)S(1)} %fusion.26, bf16[512,4,128,1]{2,1,0,3:T(4,128)(2,1)S(1)} %bitcast.72), kind=kOutput, calls=%fused_computation.22 | convolution fusion | flops 548929280 | bytes 11174912 | tf_op jit(solution)/shard_map/tkgr,rkd->tkgd/dot_general | solution.py:56
  42.2 1.3 fusion.13
  43.5 1.5 copy.22
  45.0 2.6 broadcast_in_dim.51
  47.6 4.1 %reshape.181 = bf16[512,2048]{1,0:T(8,128)(2,1)} reshape(bf16[256,2,2048]{2,1,0:T(2,128)(2,1)} %broadcast_in_dim.51) | data formatting | bytes 4194304 | tf_op jit(solution)/shard_map/reshape | solution.py:73
  51.7 6.7 %scatter_custom_fusion = bf16[768,2048]{1,0:T(8,128)(2,1)} fusion(s32[512]{0:T(512)S(1)} %bitcast.76, bf16[512,2048]{1,0:T(8,128)(2,1)} %reshape.181, bf16[]{:T(256)} %constant.25.clone.1), kind=kCustom, calls=%fused_computation.23 | custom fusion | bytes 3146240 | tf_op jit(solution)/shard_map/scatter | solution.py:80
  58.4 76.1 %all_to_all.15 = bf16[4,192,2048]{2,1,0:T(8,128)(2,1)} all-to-all(bf16[4,192,2048]{2,1,0:T(8,128)(2,1)} %bitcast.68), channel_id=1, replica_groups=mesh['grp'=4,'ep'=4,'sq'=2] {'ep'}, dimensions={0} | all-to-all | bytes 6291456 | tf_op jit(solution)/shard_map/all_to_all | solution.py:88
  134.6 0.0 all-gather.3.cloned.1.call-update
  134.6 0.0 all-gather.5.cloned.1.call-start
  134.6 0.6 copy-done.4
  135.2 0.1 copy.23
  135.4 0.1 mul.89
  135.5 0.1 copy-done.2
  135.6 2.0 broadcast_in_dim.53
  137.6 3.8 %convert_element_type.40 = f32[512,1024]{1,0:T(8,128)} reshape(f32[256,2,1024]{2,1,0:T(2,128)} %broadcast_in_dim.53) | data formatting | bytes 4194304 | tf_op jit(solution)/shard_map/convert_element_type | solution.py:75
  141.4 5.3 %scatter_custom_fusion.1 = bf16[768,1024]{1,0:T(8,128)(2,1)} fusion(s32[512]{0:T(512)S(1)} %bitcast.77, f32[512,1024]{1,0:T(8,128)} %convert_element_type.40, f32[512]{0:T(512)S(1)} %mul.89, bf16[]{:T(256)} %constant.25.clone.1), kind=kCustom, calls=%fused_computation.25 | custom fusion | flops 1048576 | bytes 3672066 | tf_op jit(solution)/shard_map/scatter | solution.py:83
  146.7 40.9 %all_to_all.16 = bf16[4,192,1024]{2,1,0:T(8,128)(2,1)} all-to-all(bf16[4,192,1024]{2,1,0:T(8,128)(2,1)} %bitcast.70), channel_id=1, replica_groups=mesh['grp'=4,'ep'=4,'sq'=2] {'ep'}, dimensions={0} | all-to-all | bytes 3145728 | tf_op jit(solution)/shard_map/all_to_all | solution.py:89
  187.5 0.0 all-gather.5.cloned.1.call-update
  187.6 0.0 reduce-scatter.2.cloned.1.call-start
  187.6 25.6 %all-gather.3.cloned.1.call-done = bf16[1536,2048]{1,0:T(8,128)(2,1)} async-done(((bf16[768,2048]{1,0:T(8,128)(2,1)}), bf16[1536,2048]{1,0:T(8,128)(2,1)}) %all-gather.3.cloned.1.call-update) | async-done | bytes 6291472 | tf_op jit(solution)/shard_map/all_gather | solution.py:97
  213.2 8.5 %fusion.9 = f32[1536,512]{1,0:T(8,128)} fusion(bf16[1536,2048]{1,0:T(8,128)(2,1)} %all-gather.3.cloned.1.call-done, bf16[1,2048,512]{2,1,0:T(8,128)(2,1)} %param.16), kind=kOutput, calls=%fused_computation.14 | convolution fusion | flops 3221225472 | bytes 11534336 | tf_op jit(solution)/shard_map/dot_general | solution.py:14
  221.8 38.0 %all-gather.5.cloned.1.call-done = bf16[1536,1024]{1,0:T(8,128)(2,1)} async-done(((bf16[768,1024]{1,0:T(8,128)(2,1)}), bf16[1536,1024]{1,0:T(8,128)(2,1)}) %all-gather.5.cloned.1.call-update) | async-done | bytes 3145744 | tf_op jit(solution)/shard_map/all_gather | solution.py:98
  259.7 14.6 %fusion.8 = bf16[1,2048,512]{2,1,0:T(8,128)(2,1)} fusion(bf16[1536,2048]{1,0:T(8,128)(2,1)} %all-gather.3.cloned.1.call-done, f32[1536,512]{1,0:T(8,128)} %fusion.9, bf16[1,2048,512]{2,1,0:T(8,128)(2,1)S(1)} %copy-done, bf16[1536,1024]{1,0:T(8,128)(2,1)} %all-gather.5.cloned.1.call-done, s32[]{:T(128)S(6)} %select_n.44), kind=kOutput, calls=%fused_computation.13 | convolution fusion | flops 6452150272 | bytes 21495812 | tf_op jit(solution)/shard_map/dot_general | solution.py:19
  274.3 0.0 reduce-scatter.2.cloned.1.call-update
  274.4 31.6 %reduce-scatter.2.cloned.1.call-done = bf16[1,512,512]{2,1,0:T(8,128)(2,1)} async-done(((bf16[1,2048,512]{2,1,0:T(8,128)(2,1)}), bf16[1,512,512]{2,1,0:T(8,128)(2,1)}) %reduce-scatter.2.cloned.1.call-update) | async-done | bytes 524304 | tf_op jit(solution)/shard_map/reduce_scatter | solution.py:101
  305.9 2.1 convert_element_type.46
  (15 shorter events, 0.1 us)
Async XLA Ops:
  6.5 253.2 %copy-start = (bf16[1,2048,512]{2,1,0:T(8,128)(2,1)S(1)}, bf16[1,2048,512]{2,1,0:T(8,128)(2,1)}, u32[]{:S(2)}) copy-start(bf16[1,2048,512]{2,1,0:T(8,128)(2,1)} %param.17) | copy-start | bytes 6291460
  8.6 27.6 %all-to-all-start = ((bf16[2,256,512]{2,1,0:T(8,128)(2,1)}), bf16[2,256,512]{2,1,0:T(8,128)(2,1)}, u32[]{:S(2)}, u32[]{:S(2)}) async-start(bf16[2,256,512]{2,1,0:T(8,128)(2,1)} %pad_maximum_fusion), calls=%async_computation | async-start | bytes 1048576 | tf_op jit(solution)/shard_map/all_to_all | solution.py:39
  12.8 200.4 %all-gather.3.cloned.1.call-start = ((), (), s32[]{:S(2)}) async-start(), calls=%async_computation.4 | async-start | bytes 9437184 | tf_op jit(solution)/shard_map/all_gather | solution.py:97
  32.7 3.2 %copy-start.1 = (f32[4,512,256,4]{2,1,3,0:T(8,128)}, f32[4,512,256,4]{2,1,3,0:T(8,128)S(1)}, u32[]{:S(2)}) copy-start(f32[4,512,256,4]{2,1,3,0:T(8,128)S(1)} %get-tuple-element.6) | copy-start | bytes 25165828
  37.4 4.8 %copy-start.3 = (f32[2048]{0:T(1024)S(1)}, f32[2048]{0:T(1024)}, u32[]{:S(2)}) copy-start(f32[2048]{0:T(1024)} %param.12) | copy-start | bytes 24580
  134.6 0.7 copy-start.4
  134.6 1.1 copy-start.2
  134.6 125.1 %all-gather.5.cloned.1.call-start = ((), (), s32[]{:S(2)}) async-start(), calls=%async_computation.5 | async-start | bytes 4718592 | tf_op jit(solution)/shard_map/all_gather | solution.py:98
  187.6 118.4 %reduce-scatter.2.cloned.1.call-start = ((), (), s32[]{:S(2)}) async-start(), calls=%async_computation.6 | async-start | bytes 2621440 | tf_op jit(solution)/shard_map/reduce_scatter | solution.py:101
Sparse Core Ops, SparseCore 0:
  134.7 78.4 all-gather.2
  214.8 44.9 all-gather.4
  274.5 31.4 reduce-scatter.1
